TPU v7x, 32 devices: a whole 2x2x4 slice. The times are simulated.
32 devices in a mesh: dp: 4 (over y, x), section: 2 (over core), ctx: 4 (over z).
Axes of the slice: x: 2, y: 2, z: 4, core: 2. Of those that a mesh axis runs over, the one named last changes fastest.
Arguments:
- queries: bfloat16 [4, 2, 512, 2048], P('dp', 'section', 'ctx'), may hold values from -6 to 6
- key_rows: bfloat16 [4, 2, 512, 128], P('dp', 'section', 'ctx'), may hold values from -6 to 6
- value_rows: bfloat16 [4, 2, 512, 128], P('dp', 'section', 'ctx'), may hold values from -6 to 6
- out_grad: bfloat16 [4, 2, 512, 2048], P('dp', 'section', 'ctx'), may hold values from -6 to 6
- attn_out: bfloat16 [4, 2, 512, 2048], P('dp', 'section', 'ctx'), may hold values from -1.796875 to 1.796875
- log_norm: float32 [4, 2, 512, 16], P('dp', 'section', 'ctx'), may hold values from 2 to 5
- selected: int32 [4, 2, 8, 16], P('dp', 'section', 'ctx'), may hold values from -1 to 7, as said below
- gate_weight: float32 [2, 16, 128], P('section'), may hold values from -0.5 to 0.5
- gate_bias: float32 [2, 16], P('section'), may hold values from -2 to 2
Outputs:
- query_grad_prev: bfloat16 [4, 2, 512, 2048], P('dp', 'section', 'ctx')
- key_grad_prev: bfloat16 [4, 2, 512, 128], P('dp', 'section', 'ctx')
- value_grad_prev: bfloat16 [4, 2, 512, 128], P('dp', 'section', 'ctx')
- gate_weight_grad: float32 [2, 16, 128], P('section')
- gate_bias_grad: float32 [2, 16], P('section')
Inputs may be any that keep to these rules, and one draw needn't show every extreme that they name: `selected`: each row of block b lists distinct blocks of 0 to b, always b itself and block 0, min(16, b + 1) of them, followed by -1 entries.
All inputs are finite; a program needn't handle non-finite values.
Results may differ from a plain program's by a relative error of at most 0.013.
Values may be sent and summed in bfloat16 or wider, within the bound.
No kernel may reach another device: no remote copies, remote signals or barrier semaphores. Data moves between devices by JAX's collectives and lax.ppermute only.
A program may use at most 64 MiB of HBM per device.

v0:
```python
import jax
import jax.numpy as jnp
from jax import lax
from jax.sharding import PartitionSpec as P

BLK = 64
SEL = 16


def from_behind(block, axis, distance):
    devices = range(lax.axis_size(axis))
    route = [(i - distance, i) for i in devices if i - distance in devices]
    return lax.ppermute(block, axis, route)


def block_grads(query_blk, grad_blk, delta_blk, norm_blk, allowed, key_part, value_part, factor):
    scores = jnp.dot(query_blk, key_part.T, preferred_element_type=jnp.float32) * factor
    probs = jnp.where(allowed, jnp.exp(jnp.where(allowed, scores - norm_blk[:, None], 0.0)), 0.0)
    probs_b = probs.astype(jnp.bfloat16)
    dprobs = jnp.dot(grad_blk, value_part.T, preferred_element_type=jnp.float32)
    dscores = (probs * (dprobs - delta_blk[:, None])).astype(jnp.bfloat16)
    query_part = factor * jnp.dot(dscores, key_part, preferred_element_type=jnp.float32)
    key_part_grad = factor * jnp.dot(dscores.T, query_blk, preferred_element_type=jnp.float32)
    value_part_grad = jnp.dot(probs_b.T, grad_blk, preferred_element_type=jnp.float32)
    return (query_part, key_part_grad, value_part_grad)


def on_device(
    queries, key_rows, value_rows, out_grad, attn_out, log_norm, selected, gate_weight, gate_bias
):
    query_mat = queries[0, 0]
    length_dev = query_mat.shape[0]
    head_count = gate_weight.shape[1]
    head_dim = gate_weight.shape[2]
    local_blocks = length_dev // BLK
    chosen = selected[0, 0]
    own_keys = key_rows[0, 0]
    own_values = value_rows[0, 0]
    weight = gate_weight[0]
    factor = head_dim ** (-0.5)
    rank_ctx = lax.axis_index("ctx")
    seq_len = length_dev * lax.axis_size("ctx")
    nblocks = seq_len // BLK
    query3 = query_mat.reshape(length_dev, head_count, head_dim).astype(jnp.float32)
    gate = jax.nn.sigmoid(jnp.sum(query3 * weight[None], axis=-1) + gate_bias[0][None])
    grad3 = out_grad[0, 0].reshape(length_dev, head_count, head_dim).astype(jnp.float32)
    output3 = attn_out[0, 0].reshape(length_dev, head_count, head_dim).astype(jnp.float32)
    branch_grad = (gate[:, :, None] * grad3).astype(jnp.bfloat16)
    row_delta = jnp.sum(branch_grad.astype(jnp.float32) * output3, axis=-1)
    pre_grad = jnp.sum(grad3 * output3, axis=-1) * gate * (1.0 - gate)
    rows_total = length_dev * head_count
    query_flat = query_mat.reshape(rows_total, head_dim)
    grad_flat = branch_grad.reshape(rows_total, head_dim)
    delta_flat = row_delta.reshape(-1)
    norm_flat = log_norm[0, 0].reshape(-1)
    query_pos = rank_ctx * length_dev + jnp.arange(rows_total, dtype=jnp.int32) // head_count
    gate_term = (pre_grad[:, :, None] * weight[None]).reshape(rows_total, head_dim)
    key_all, value_all = (
        lax.all_gather(own_keys, "ctx", axis=0, tiled=True),
        lax.all_gather(own_values, "ctx", axis=0, tiled=True),
    )
    safe_ids = jnp.maximum(chosen, 0)
    key_slots = key_all.reshape(nblocks, BLK, head_dim)[safe_ids].reshape(
        local_blocks, SEL * BLK, head_dim
    )
    value_slots = value_all.reshape(nblocks, BLK, head_dim)[safe_ids].reshape(
        local_blocks, SEL * BLK, head_dim
    )
    block_rows = BLK * head_count

    def one_block(items):
        query_blk, grad_blk, delta_blk, norm_blk, pos_blk, chosen_row, key_part, value_part = items
        key_pos = (
            jnp.maximum(chosen_row, 0)[:, None] * BLK + jnp.arange(BLK, dtype=jnp.int32)[None, :]
        ).reshape(-1)
        usable = jnp.repeat(chosen_row >= 0, BLK)
        allowed = usable[None, :] & (key_pos[None, :] <= pos_blk[:, None])
        return block_grads(
            query_blk, grad_blk, delta_blk, norm_blk, allowed, key_part, value_part, factor
        )

    items = (
        query_flat.reshape(local_blocks, block_rows, head_dim),
        grad_flat.reshape(local_blocks, block_rows, head_dim),
        delta_flat.reshape(local_blocks, block_rows),
        norm_flat.reshape(local_blocks, block_rows),
        query_pos.reshape(local_blocks, block_rows),
        chosen,
        key_slots,
        value_slots,
    )
    query_blocks, key_slot_grad, value_slot_grad = lax.map(one_block, items)
    query_acc = query_blocks.reshape(rows_total, head_dim)
    slot_count = local_blocks * SEL
    both_slots = jnp.concatenate(
        [
            key_slot_grad.reshape(slot_count, BLK, head_dim),
            value_slot_grad.reshape(slot_count, BLK, head_dim),
        ],
        axis=-1,
    ).reshape(slot_count, BLK * 2 * head_dim)
    flat_ids = chosen.reshape(-1)
    block_ids = jnp.arange(seq_len // BLK, dtype=jnp.int32)
    one_hot = (flat_ids[None, :] == block_ids[:, None]).astype(jnp.float32)
    placed = jnp.dot(
        one_hot, both_slots, precision=lax.Precision.HIGHEST, preferred_element_type=jnp.float32
    )
    both_full = placed.reshape(seq_len, 2 * head_dim)
    both_mine = lax.psum_scatter(both_full, "ctx", scatter_dimension=0, tiled=True)
    key_mine = both_mine[:, :head_dim]
    value_mine = both_mine[:, head_dim:]
    query_grad = (
        (query_acc + gate_term).astype(jnp.bfloat16).reshape(length_dev, head_count * head_dim)
    )
    query_sent, key_sent, value_sent = from_behind(
        (query_grad, key_mine.astype(jnp.bfloat16), value_mine.astype(jnp.bfloat16)), "section", -1
    )
    weight_local = jnp.sum(pre_grad[:, :, None] * query3, axis=0)
    bias_local = jnp.sum(pre_grad, axis=0)
    weight_total, bias_total = lax.psum((weight_local, bias_local), ("dp", "ctx"))
    return (
        query_sent[None, None],
        key_sent[None, None],
        value_sent[None, None],
        weight_total[None],
        bias_total[None],
    )


def solution(mesh):
    return jax.shard_map(
        on_device,
        mesh=mesh,
        in_specs=(
            P("dp", "section", "ctx", None),
            P("dp", "section", "ctx", None),
            P("dp", "section", "ctx", None),
            P("dp", "section", "ctx", None),
            P("dp", "section", "ctx", None),
            P("dp", "section", "ctx", None),
            P("dp", "section", "ctx", None),
            P("section", None, None),
            P("section", None),
        ),
        out_specs=(
            P("dp", "section", "ctx", None),
            P("dp", "section", "ctx", None),
            P("dp", "section", "ctx", None),
            P("section", None, None),
            P("section", None),
        ),
        check_vma=False,
    )
```

profile of v0, /device:TPU:0, one launch (start us, length us, event | category | flops | bytes accessed | tf_op | source)
XLA Modules:
  0.0 151.8 jit_solution(7226072562469080117)
XLA Ops:
  7.2 0.8 eq.15
  8.0 0.7 broadcast_maximum_fusion
  8.7 2.2 %convert_bitcast_fusion.2 = f32[16,8,16,128]{3,1,2,0:T(8,128)} fusion(bf16[1,1,128,2048]{3,2,1,0:T(8,128)(2,1)} %param.14), kind=kLoop, calls=%fused_computation.56 | loop fusion | flops 262144 | bytes 1572864
  10.9 1.3 reshape.184
  12.2 1.3 reshape_reshape_squeeze.6
  13.6 0.2 copy.25
  13.8 0.3 multiply_reduce_fusion.2
  14.8 15.1 %all-gather = bf16[1,1,512,128]{3,2,1,0:T(8,128)(2,1)S(1)} all-gather(bf16[1,1,128,128]{3,2,1,0:T(8,128)(2,1)S(1)} %copy-done.10), channel_id=2, replica_groups=mesh['dp'=4,'section'=2,'ctx'=4] {'ctx'}, dimensions={2}, use_global_device_ids=true | all-gather | bytes 163840 | tf_op jit(solution)/shard_map/all_gather | solution.py:59
  29.9 13.5 %all-gather.1 = bf16[1,1,512,128]{3,2,1,0:T(8,128)(2,1)S(1)} all-gather(bf16[1,1,128,128]{3,2,1,0:T(8,128)(2,1)S(1)} %copy-done.11), channel_id=3, replica_groups=mesh['dp'=4,'section'=2,'ctx'=4] {'ctx'}, dimensions={2}, use_global_device_ids=true | all-gather | bytes 163840 | tf_op jit(solution)/shard_map/all_gather | solution.py:60
  43.4 1.4 gather_fusion.1
  44.8 0.6 gather_fusion
  45.6 1.2 copy.27
  46.8 1.2 copy.26
  48.1 2.5 %multiply_reduce_fusion = (f32[128,16]{1,0:T(8,128)S(1)}, f32[128,16]{1,0:T(8,128)S(1)}) fusion(f32[128,16,128]{2,1,0:T(8,128)} %bitcast.126, f32[128,16,128]{2,1,0:T(8,128)} %bitcast.125, f32[128,16]{1,0:T(8,128)S(1)} %copy.22), kind=kLoop, calls=%fused_computation.51 | loop fusion | flops 1830912 | bytes 2121728 | tf_op jit(solution)/shard_map/reduce_sum | solution.py:50
  50.7 0.3 multiply_convert_fusion.2
  51.0 18.5 %while.14 = (s32[]{:T(128)}, f32[2,1024,128]{2,1,0:T(8,128)}, f32[2,1024,128]{2,1,0:T(8,128)}, f32[2,1024,128]{2,1,0:T(8,128)}, s32[2,16]{1,0:T(2,128)S(1)}, /*i...) while((s32[]{:T(128)}, f32[2,1024,128]{2,1,0:T(8,128)}, ...), condition=%wide.region_3.4_spmd, body=%wide.region_2.0_spmd.sunk | while | flops 1359217664 | bytes 41232960 | solution.py:92
  51.4 0.7 fusion.70
  52.2 2.6 %fusion.73 = f32[2,1024,128]{2,1,0:T(8,128)} fusion(f32[2,1024,128]{2,1,0:T(8,128)} %get-tuple-element.199, s32[]{:T(128)S(6)} %copy.38, f32[1024,1024]{1,0:T(8,128)S(1)} %fusion.70, f32[1024]{0:T(1024)S(1)} %bitcast.135, s32[1024]{0:T(1024)S(1)} %add.124, s32[1024]{0:T(1024)S(1)} %bitcast.132, pred[1024]{0:T(1024)(128)(4,1)S(1)} %and.48, ...), kind=kOutput, calls=%fused_computation.7.clone.1 | convolution fusion | flops 275775488 | bytes 4995072 | tf_op jit(solution)/shard_map/while/body/eval_jaxpr/dot_general | solution.py:24
  54.8 2.2 %multiply_convert_fusion.4 = bf16[1024,1024]{1,0:T(8,128)(2,1)S(1)} fusion(f32[1024,1024]{1,0:T(8,128)S(1)} %fusion.70, f32[1024]{0:T(1024)S(1)} %bitcast.134, f32[1024]{0:T(1024)S(1)} %bitcast.136, s32[1024]{0:T(1024)S(1)} %add.124, s32[1024]{0:T(1024)S(1)} %bitcast.133, pred[1024]{0:T(1024)(128)(4,1)S(1)} %and.48, ...), kind=kOutput, calls=%fused_computation.2.clone.1 | convolution fusion | flops 277872640 | bytes 6834176 | tf_op jit(solution)/shard_map/while/body/eval_jaxpr/dot_general | solution.py:20
  57.1 0.8 fusion.72
  57.8 0.4 copy-done.2
  58.3 0.7 fusion.71
  59.0 0.3 copy-done.6
  59.3 1.0 copy-done.3
  60.6 0.7 fusion.70
  61.4 2.6 %fusion.73 = f32[2,1024,128]{2,1,0:T(8,128)} fusion(f32[2,1024,128]{2,1,0:T(8,128)} %get-tuple-element.199, s32[]{:T(128)S(6)} %copy.38, f32[1024,1024]{1,0:T(8,128)S(1)} %fusion.70, f32[1024]{0:T(1024)S(1)} %bitcast.135, s32[1024]{0:T(1024)S(1)} %add.124, s32[1024]{0:T(1024)S(1)} %bitcast.132, pred[1024]{0:T(1024)(128)(4,1)S(1)} %and.48, ...), kind=kOutput, calls=%fused_computation.7.clone.1 | convolution fusion | flops 275775488 | bytes 4995072 | tf_op jit(solution)/shard_map/while/body/eval_jaxpr/dot_general | solution.py:24
  64.0 2.3 %multiply_convert_fusion.4 = bf16[1024,1024]{1,0:T(8,128)(2,1)S(1)} fusion(f32[1024,1024]{1,0:T(8,128)S(1)} %fusion.70, f32[1024]{0:T(1024)S(1)} %bitcast.134, f32[1024]{0:T(1024)S(1)} %bitcast.136, s32[1024]{0:T(1024)S(1)} %add.124, s32[1024]{0:T(1024)S(1)} %bitcast.133, pred[1024]{0:T(1024)(128)(4,1)S(1)} %and.48, ...), kind=kOutput, calls=%fused_computation.2.clone.1 | convolution fusion | flops 277872640 | bytes 6834176 | tf_op jit(solution)/shard_map/while/body/eval_jaxpr/dot_general | solution.py:20
  66.3 0.8 fusion.72
  67.0 0.4 copy-done.2
  67.5 0.7 fusion.71
  68.2 0.3 copy-done.6
  68.5 1.0 copy-done.3
  69.5 1.7 %pad_maximum_fusion = f32[32,64,256]{2,1,0:T(8,128)S(1)} fusion(f32[32,64,128]{2,1,0:T(8,128)} %bitcast.22, f32[32,64,128]{2,1,0:T(8,128)} %bitcast.130), kind=kLoop, calls=%fused_computation.43 | loop fusion | flops 524288 | bytes 4194304 | tf_op jit(solution)/shard_map/concatenate | solution.py:95
  71.2 1.2 copy.29
  72.4 0.8 fusion.39
  73.3 0.9 reshape.181
  74.2 0.2 fusion.41
  74.7 0.3 mul.125
  75.0 0.5 fusion.37
  75.5 1.3 collective-permute-start
  77.0 20.3 %reduce-scatter.2.cloned.1.call-done = f32[128,256]{1,0:T(8,128)} async-done(((f32[512,256]{1,0:T(8,128)}), f32[128,256]{1,0:T(8,128)}) %reduce-scatter.2.cloned.1.call-update) | async-done | bytes 131088 | tf_op jit(solution)/shard_map/reduce_scatter | solution.py:109
  97.3 0.9 convert.8
  98.2 1.3 collective-permute-start.2
  99.5 1.3 collective-permute-start.1
  100.9 40.9 %all-reduce = (f32[1,16,128]{2,1,0:T(8,128)}, f32[1,16]{1,0:T(1,128)}) all-reduce(f32[1,16,128]{2,1,0:T(8,128)S(1)} %bitcast.139, f32[1,16]{1,0:T(1,128)S(1)} %bitcast.145), channel_id=1, replica_groups=mesh['dp'=4,'section'=2,'ctx'=4] {'dp','ctx'}, use_global_device_ids=true, to_apply=%region_7.8 | all-reduce | flops 2064 | bytes 16512 | tf_op jit(solution)/shard_map/psum | solution.py:120
  141.8 1.9 %copy.51 = bf16[1,1,128,2048]{3,2,1,0:T(8,128)(2,1)} copy(bf16[1,1,128,2048]{3,2,1,0:T(8,128)(2,1)} %bitcast.20) | data formatting | bytes 1048576
  143.7 0.6 copy.52
  144.3 0.6 copy.53
  (79 shorter events, 2.5 us)
Async XLA Ops:
  7.2 6.3 %copy-start = (bf16[1,1,128,2048]{3,2,1,0:T(8,128)(2,1)S(1)}, bf16[1,1,128,2048]{3,2,1,0:T(8,128)(2,1)}, u32[]{:S(2)}) copy-start(bf16[1,1,128,2048]{3,2,1,0:T(8,128)(2,1)} %param.11) | copy-start | bytes 1572868
  7.2 6.7 %copy-start.9 = (f32[1,16,128]{2,1,0:T(8,128)S(1)}, f32[1,16,128]{2,1,0:T(8,128)}, u32[]{:S(2)}) copy-start(f32[1,16,128]{2,1,0:T(8,128)} %param.18) | copy-start | bytes 24580
  7.2 90.1 %reduce-scatter.2.cloned.1.call-start = ((), (), s32[]{:S(2)}) async-start(), calls=%async_computation.1 | async-start | bytes 655360 | tf_op jit(solution)/shard_map/reduce_scatter | solution.py:109
  8.7 5.8 %copy-start.12 = (f32[1,1,128,16]{2,3,1,0:T(8,128)S(1)}, f32[1,1,128,16]{2,3,1,0:T(8,128)}, u32[]{:S(2)}) copy-start(f32[1,1,128,16]{2,3,1,0:T(8,128)} %param.16) | copy-start | bytes 24580
  10.9 3.8 %copy-start.13 = (f32[1,16]{1,0:T(1,128)S(1)}, f32[1,16]{1,0:T(1,128)}, u32[]{:S(2)}) copy-start(f32[1,16]{1,0:T(1,128)} %param.19) | copy-start | bytes 196
  10.9 4.0 %copy-start.10 = (bf16[1,1,128,128]{3,2,1,0:T(8,128)(2,1)S(1)}, bf16[1,1,128,128]{3,2,1,0:T(8,128)(2,1)}, u32[]{:S(2)}) copy-start(bf16[1,1,128,128]{3,2,1,0:T(8,128)(2,1)} %param.12) | copy-start | bytes 98308
  10.9 19.0 %copy-start.11 = (bf16[1,1,128,128]{3,2,1,0:T(8,128)(2,1)S(1)}, bf16[1,1,128,128]{3,2,1,0:T(8,128)(2,1)}, u32[]{:S(2)}) copy-start(bf16[1,1,128,128]{3,2,1,0:T(8,128)(2,1)} %param.13) | copy-start | bytes 98308
  12.2 33.3 %copy-start.7 = (bf16[1,1,128,2048]{3,2,1,0:T(8,128)(2,1)S(1)}, bf16[1,1,128,2048]{3,2,1,0:T(8,128)(2,1)}, u32[]{:S(2)}) copy-start(bf16[1,1,128,2048]{3,2,1,0:T(8,128)(2,1)} %param.15) | copy-start | bytes 1572868
  45.5 1.3 copy-start.1
  45.6 5.5 %copy-start.14 = (s32[1,1,2,16]{3,2,1,0:T(2,128)S(1)}, s32[1,1,2,16]{3,2,1,0:T(2,128)}, u32[]{:S(2)}) copy-start(s32[1,1,2,16]{3,2,1,0:T(2,128)} %param.17) | copy-start | bytes 388
  52.1 2.6 %copy-start.8 = (bf16[2,1024,128]{2,1,0:T(8,128)(2,1)S(1)}, bf16[2,1024,128]{2,1,0:T(8,128)(2,1)}, u32[]{:S(2)}) copy-start(bf16[2,1024,128]{2,1,0:T(8,128)(2,1)} %get-tuple-element.219) | copy-start | bytes 1572868 | tf_op jit(solution)/shard_map/while
  54.8 2.3 %copy-start.5 = (f32[2,1024,128]{2,1,0:T(8,128)S(1)}, f32[2,1024,128]{2,1,0:T(8,128)}, u32[]{:S(2)}) copy-start(f32[2,1024,128]{2,1,0:T(8,128)} %get-tuple-element.198) | copy-start | bytes 3145732 | tf_op jit(solution)/shard_map/while
  57.0 1.2 copy-start.2
  58.3 1.0 copy-start.6
  59.3 1.0 copy-start.3
  61.4 2.6 %copy-start.8 = (bf16[2,1024,128]{2,1,0:T(8,128)(2,1)S(1)}, bf16[2,1024,128]{2,1,0:T(8,128)(2,1)}, u32[]{:S(2)}) copy-start(bf16[2,1024,128]{2,1,0:T(8,128)(2,1)} %get-tuple-element.219) | copy-start | bytes 1572868 | tf_op jit(solution)/shard_map/while
  64.0 2.3 %copy-start.5 = (f32[2,1024,128]{2,1,0:T(8,128)S(1)}, f32[2,1024,128]{2,1,0:T(8,128)}, u32[]{:S(2)}) copy-start(f32[2,1024,128]{2,1,0:T(8,128)} %get-tuple-element.198) | copy-start | bytes 3145732 | tf_op jit(solution)/shard_map/while
  66.3 1.2 copy-start.2
  67.5 1.0 copy-start.6
  68.5 1.0 copy-start.3
  71.2 3.3 %copy-start.4 = (f32[2,1024,128]{2,1,0:T(8,128)S(1)}, f32[2,1024,128]{2,1,0:T(8,128)}, u32[]{:S(2)}) copy-start(f32[2,1024,128]{2,1,0:T(8,128)} %get-tuple-element.69) | copy-start | bytes 3145732
  75.5 66.3 %collective-permute-start = (bf16[128,2048]{1,0:T(8,128)(2,1)S(1)}, bf16[128,2048]{1,0:T(8,128)(2,1)}, u32[]{:S(2)}, u32[]{:S(2)}) collective-permute-start(bf16[128,2048]{1,0:T(8,128)(2,1)S(1)} %fusion.37), channel_id=1, source_target_pairs={{4,0},{5,1},{6,2},{7,3},{12,8},{13,9},{14,10},{15,11},{20,16},{21,... | collective-permute-start | bytes 1572872 | tf_op jit(solution)/shard_map/ppermute | solution.py:13
  98.2 43.6 %collective-permute-start.2 = (bf16[128,128]{1,0:T(8,128)(2,1)S(1)}, bf16[128,128]{1,0:T(8,128)(2,1)S(1)}, u32[]{:S(2)}, u32[]{:S(2)}) collective-permute-start(bf16[128,128]{1,0:T(8,128)(2,1)S(1)} %get-tuple-element.104), channel_id=1, source_target_pairs={{4,0},{5,1},{6,2},{7,3},{12,8},{13,9},{14,10},{15,11},{20,16},{21,... | collective-permute-start | bytes 98312 | tf_op jit(solution)/shard_map/ppermute | solution.py:13
  99.5 42.3 %collective-permute-start.1 = (bf16[128,128]{1,0:T(8,128)(2,1)S(1)}, bf16[128,128]{1,0:T(8,128)(2,1)S(1)}, u32[]{:S(2)}, u32[]{:S(2)}) collective-permute-start(bf16[128,128]{1,0:T(8,128)(2,1)S(1)} %get-tuple-element.105), channel_id=1, source_target_pairs={{4,0},{5,1},{6,2},{7,3},{12,8},{13,9},{14,10},{15,11},{20,16},{21,... | collective-permute-start | bytes 98312 | tf_op jit(solution)/shard_map/ppermute | solution.py:13
Sparse Core Ops, SparseCore 0:
  74.3 22.9 reduce-scatter.1
where the time goes:
time: 152 us
  blocking collectives  69.4 us (46%)
  waiting for transfers between devices  20.3 us (13%)
  local copies, waits for them, and re-layouts  18.8 us (12%)
  matrix products  14.9 us (10%)
  between operations  14.4 us (9%)
  other arithmetic  9.91 us (7%)
  starting transfers between devices  3.91 us (3%)
    psum x1, blocking collectives, on_device(): lax.psum((weight_local, bias_local), ('dp', 'ctx'))  40.9 us
    reduce_scatter x1, waiting for transfers between devices, on_device(): lax.psum_scatter(both_full, 'ctx', scatter_dimension=0, tiled=True)  20.3 us
    all_gather x1, blocking collectives, on_device(): lax.all_gather(own_keys, 'ctx', axis=0, tiled=True)  15.1 us
    all_gather x1, blocking collectives, on_device(): lax.all_gather(own_values, 'ctx', axis=0, tiled=True)  13.5 us
    unnamed x28, local copies, waits for them, and re-layouts  7 us
    dot_general x2, matrix products, block_grads(): jnp.dot(probs_b.T, grad_blk, preferred_element_type=jnp.float32)  5.24 us
    dot_general x2, matrix products, block_grads(): dprobs = jnp.dot(grad_blk, value_part.T, preferred_element_type=jnp.float32)  4.5 us
    ppermute x3, starting transfers between devices, from_behind(): return lax.ppermute(block, axis, route)  3.88 us
  transfers between devices with their start and end apart: 4, of which 1 were waited for; matrix products, arithmetic and copies ran while one was open for 2% of the time, Pallas kernels for 0%

commit v1 on v0

--- a/solution.py
+++ b/solution.py
@@ -5,6 +5,11 @@
 
 BLK = 64
 SEL = 16
+
+
+def one_after_other(value, one, other):
+    inner = lax.psum(value, one)
+    return lax.psum(inner, other)
 
 
 def from_behind(block, axis, distance):
@@ -117,7 +122,7 @@
     )
     weight_local = jnp.sum(pre_grad[:, :, None] * query3, axis=0)
     bias_local = jnp.sum(pre_grad, axis=0)
-    weight_total, bias_total = lax.psum((weight_local, bias_local), ("dp", "ctx"))
+    weight_total, bias_total = one_after_other((weight_local, bias_local), "ctx", "dp")
     return (
         query_sent[None, None],
         key_sent[None, None],

time: 152 us -> 131 us (0.86)
  blocking collectives: 69.4 us -> 48.5 us
    psum x1 -> x2, blocking collectives: 40.9 us -> 19.9 us  [the longest x1 10.8 us: one_after_other(): return lax.psum(inner, other)]
where the time goes in v1:
time: 131 us
  blocking collectives  48.5 us (37%)
  waiting for transfers between devices  20.3 us (15%)
  local copies, waits for them, and re-layouts  18.7 us (14%)
  matrix products  14.9 us (11%)
  between operations  14.4 us (11%)
  other arithmetic  9.9 us (8%)
  starting transfers between devices  3.91 us (3%)
    reduce_scatter x1, waiting for transfers between devices, on_device(): lax.psum_scatter(both_full, 'ctx', scatter_dimension=0, tiled=True)  20.3 us
    all_gather x1, blocking collectives, on_device(): lax.all_gather(own_keys, 'ctx', axis=0, tiled=True)  15.1 us
    all_gather x1, blocking collectives, on_device(): lax.all_gather(own_values, 'ctx', axis=0, tiled=True)  13.5 us
    psum x1, blocking collectives, one_after_other(): return lax.psum(inner, other)  10.8 us
    psum x1, blocking collectives, one_after_other(): inner = lax.psum(value, one)  9.16 us
    unnamed x28, local copies, waits for them, and re-layouts  7 us
    dot_general x2, matrix products, block_grads(): jnp.dot(probs_b.T, grad_blk, preferred_element_type=jnp.float32)  5.23 us
    dot_general x2, matrix products, block_grads(): dprobs = jnp.dot(grad_blk, value_part.T, preferred_element_type=jnp.float32)  4.5 us
  transfers between devices with their start and end apart: 4, of which 1 were waited for; matrix products, arithmetic and copies ran while one was open for 2% of the time, Pallas kernels for 0%

profile of v1, /device:TPU:0, one launch (start us, length us, event | category | flops | bytes accessed | tf_op | source)
XLA Modules:
  0.0 130.7 jit_solution(17942588480993108256)
XLA Ops:
  7.2 0.8 eq.15
  8.0 0.7 broadcast_maximum_fusion
  8.7 2.1 %convert_bitcast_fusion.2 = f32[16,8,16,128]{3,1,2,0:T(8,128)} fusion(bf16[1,1,128,2048]{3,2,1,0:T(8,128)(2,1)} %param.14), kind=kLoop, calls=%fused_computation.56 | loop fusion | flops 262144 | bytes 1572864
  10.9 1.3 reshape.183
  12.2 1.3 %reshape_reshape_squeeze.6 = bf16[2,1024,128]{2,1,0:T(8,128)(2,1)S(1)} reshape(bf16[1,1,128,2048]{3,2,1,0:T(8,128)(2,1)} %param.11) | data formatting | bytes 1048576 | tf_op jit(solution)/shard_map/reshape;reshape;squeeze | solution.py:88
  13.8 0.3 multiply_reduce_fusion.2
  14.8 15.1 %all-gather = bf16[1,1,512,128]{3,2,1,0:T(8,128)(2,1)S(1)} all-gather(bf16[1,1,128,128]{3,2,1,0:T(8,128)(2,1)S(1)} %copy-done.10), channel_id=2, replica_groups=mesh['dp'=4,'section'=2,'ctx'=4] {'ctx'}, dimensions={2}, use_global_device_ids=true | all-gather | bytes 163840 | tf_op jit(solution)/shard_map/all_gather | solution.py:64
  29.9 13.5 %all-gather.1 = bf16[1,1,512,128]{3,2,1,0:T(8,128)(2,1)S(1)} all-gather(bf16[1,1,128,128]{3,2,1,0:T(8,128)(2,1)S(1)} %copy-done.11), channel_id=3, replica_groups=mesh['dp'=4,'section'=2,'ctx'=4] {'ctx'}, dimensions={2}, use_global_device_ids=true | all-gather | bytes 163840 | tf_op jit(solution)/shard_map/all_gather | solution.py:65
  43.4 1.4 %gather_fusion.1 = bf16[32,64,128]{2,1,0:T(8,128)(2,1)} fusion(bf16[8,64,128]{2,1,0:T(8,128)(2,1)S(1)} %bitcast.130, s32[1024]{0:T(1024)S(1)} %pad_clamp_fusion), kind=kCustom, calls=%fused_computation.1 | custom fusion | bytes 1048704 | tf_op jit(solution)/shard_map/gather | solution.py:71
  44.8 0.6 gather_fusion
  45.6 1.2 copy.27
  46.8 1.2 copy.26
  48.1 2.5 %multiply_reduce_fusion = (f32[128,16]{1,0:T(8,128)S(1)}, f32[128,16]{1,0:T(8,128)S(1)}) fusion(f32[128,16,128]{2,1,0:T(8,128)} %bitcast.127, f32[128,16,128]{2,1,0:T(8,128)} %bitcast.126, f32[128,16]{1,0:T(8,128)S(1)} %copy.22), kind=kLoop, calls=%fused_computation.51 | loop fusion | flops 1830912 | bytes 2121728 | tf_op jit(solution)/shard_map/reduce_sum | solution.py:55
  50.7 0.3 multiply_convert_fusion.2
  51.0 18.4 %while.14 = (s32[]{:T(128)}, f32[2,1024,128]{2,1,0:T(8,128)}, f32[2,1024,128]{2,1,0:T(8,128)}, f32[2,1024,128]{2,1,0:T(8,128)}, s32[2,16]{1,0:T(2,128)S(1)}, /*i...) while((s32[]{:T(128)}, f32[2,1024,128]{2,1,0:T(8,128)}, ...), condition=%wide.region_3.4_spmd, body=%wide.region_2.0_spmd.sunk | while | flops 1359217664 | bytes 41232960 | solution.py:97
  51.4 0.7 fusion.70
  52.1 2.6 %fusion.73 = f32[2,1024,128]{2,1,0:T(8,128)} fusion(f32[2,1024,128]{2,1,0:T(8,128)} %get-tuple-element.201, s32[]{:T(128)S(6)} %copy.38, f32[1024,1024]{1,0:T(8,128)S(1)} %fusion.70, f32[1024]{0:T(1024)S(1)} %bitcast.136, s32[1024]{0:T(1024)S(1)} %add.128, s32[1024]{0:T(1024)S(1)} %bitcast.133, pred[1024]{0:T(1024)(128)(4,1)S(1)} %and.48, ...), kind=kOutput, calls=%fused_computation.7.clone.1 | convolution fusion | flops 275775488 | bytes 4995072 | tf_op jit(solution)/shard_map/while/body/eval_jaxpr/dot_general | solution.py:29
  54.8 2.3 %multiply_convert_fusion.4 = bf16[1024,1024]{1,0:T(8,128)(2,1)S(1)} fusion(f32[1024,1024]{1,0:T(8,128)S(1)} %fusion.70, f32[1024]{0:T(1024)S(1)} %bitcast.135, f32[1024]{0:T(1024)S(1)} %bitcast.137, s32[1024]{0:T(1024)S(1)} %add.128, s32[1024]{0:T(1024)S(1)} %bitcast.134, pred[1024]{0:T(1024)(128)(4,1)S(1)} %and.48, ...), kind=kOutput, calls=%fused_computation.2.clone.1 | convolution fusion | flops 277872640 | bytes 6834176 | tf_op jit(solution)/shard_map/while/body/eval_jaxpr/dot_general | solution.py:25
  57.0 0.8 fusion.72
  57.8 0.4 copy-done.2
  58.3 0.7 fusion.71
  59.0 0.3 copy-done.6
  59.3 1.0 copy-done.3
  60.6 0.7 fusion.70
  61.3 2.6 %fusion.73 = f32[2,1024,128]{2,1,0:T(8,128)} fusion(f32[2,1024,128]{2,1,0:T(8,128)} %get-tuple-element.201, s32[]{:T(128)S(6)} %copy.38, f32[1024,1024]{1,0:T(8,128)S(1)} %fusion.70, f32[1024]{0:T(1024)S(1)} %bitcast.136, s32[1024]{0:T(1024)S(1)} %add.128, s32[1024]{0:T(1024)S(1)} %bitcast.133, pred[1024]{0:T(1024)(128)(4,1)S(1)} %and.48, ...), kind=kOutput, calls=%fused_computation.7.clone.1 | convolution fusion | flops 275775488 | bytes 4995072 | tf_op jit(solution)/shard_map/while/body/eval_jaxpr/dot_general | solution.py:29
  63.9 2.3 %multiply_convert_fusion.4 = bf16[1024,1024]{1,0:T(8,128)(2,1)S(1)} fusion(f32[1024,1024]{1,0:T(8,128)S(1)} %fusion.70, f32[1024]{0:T(1024)S(1)} %bitcast.135, f32[1024]{0:T(1024)S(1)} %bitcast.137, s32[1024]{0:T(1024)S(1)} %add.128, s32[1024]{0:T(1024)S(1)} %bitcast.134, pred[1024]{0:T(1024)(128)(4,1)S(1)} %and.48, ...), kind=kOutput, calls=%fused_computation.2.clone.1 | convolution fusion | flops 277872640 | bytes 6834176 | tf_op jit(solution)/shard_map/while/body/eval_jaxpr/dot_general | solution.py:25
  66.2 0.8 fusion.72
  67.0 0.4 copy-done.2
  67.4 0.7 fusion.71
  68.1 0.3 copy-done.6
  68.4 1.0 copy-done.3
  69.4 1.7 %pad_maximum_fusion = f32[32,64,256]{2,1,0:T(8,128)S(1)} fusion(f32[32,64,128]{2,1,0:T(8,128)} %bitcast.22, f32[32,64,128]{2,1,0:T(8,128)} %bitcast.131), kind=kLoop, calls=%fused_computation.43 | loop fusion | flops 524288 | bytes 4194304 | tf_op jit(solution)/shard_map/concatenate | solution.py:100
  71.1 1.2 copy.29
  72.4 0.8 fusion.39
  73.2 0.9 reshape.181
  74.1 0.2 fusion.41
  74.6 0.3 mul.125
  75.0 0.5 fusion.37
  75.4 1.3 collective-permute-start
  76.9 20.3 %reduce-scatter.2.cloned.1.call-done = f32[128,256]{1,0:T(8,128)} async-done(((f32[512,256]{1,0:T(8,128)}), f32[128,256]{1,0:T(8,128)}) %reduce-scatter.2.cloned.1.call-update) | async-done | bytes 131088 | tf_op jit(solution)/shard_map/reduce_scatter | solution.py:114
  97.2 0.9 convert.8
  98.1 1.3 collective-permute-start.2
  99.4 1.3 collective-permute-start.1
  100.8 9.2 %all-reduce = (f32[16,128]{1,0:T(8,128)S(1)}, f32[16]{0:T(128)S(1)}) all-reduce(f32[16,128]{1,0:T(8,128)S(1)} %bitcast.140, f32[16]{0:T(128)S(1)} %get-tuple-element.102), channel_id=1, replica_groups=mesh['dp'=4,'section'=2,'ctx'=4] {'ctx'}, use_global_device_ids=true, to_apply=%region_7.8 | all-reduce | flops 2064 | bytes 16512 | tf_op jit(solution)/shard_map/psum | solution.py:11
  110.0 10.8 %all-reduce.1 = (f32[1,16,128]{2,1,0:T(8,128)}, f32[1,16]{1,0:T(1,128)}) all-reduce(f32[1,16,128]{2,1,0:T(8,128)S(1)} %bitcast.143, f32[1,16]{1,0:T(1,128)S(1)} %bitcast.148), channel_id=1, replica_groups=mesh['dp'=4,'section'=2,'ctx'=4] {'dp'}, use_global_device_ids=true, to_apply=%region_8.9 | all-reduce | flops 2064 | bytes 16512 | tf_op jit(solution)/shard_map/psum | solution.py:12
  120.8 1.9 %copy.51 = bf16[1,1,128,2048]{3,2,1,0:T(8,128)(2,1)} copy(bf16[1,1,128,2048]{3,2,1,0:T(8,128)(2,1)} %bitcast.20) | data formatting | bytes 1048576
  122.6 0.6 copy.52
  123.3 0.6 copy.53
  (80 shorter events, 2.7 us)
Async XLA Ops:
  7.2 6.3 %copy-start = (bf16[1,1,128,2048]{3,2,1,0:T(8,128)(2,1)S(1)}, bf16[1,1,128,2048]{3,2,1,0:T(8,128)(2,1)}, u32[]{:S(2)}) copy-start(bf16[1,1,128,2048]{3,2,1,0:T(8,128)(2,1)} %param.11) | copy-start | bytes 1572868
  7.2 6.6 %copy-start.9 = (f32[1,16,128]{2,1,0:T(8,128)S(1)}, f32[1,16,128]{2,1,0:T(8,128)}, u32[]{:S(2)}) copy-start(f32[1,16,128]{2,1,0:T(8,128)} %param.18) | copy-start | bytes 24580
  7.2 90.0 %reduce-scatter.2.cloned.1.call-start = ((), (), s32[]{:S(2)}) async-start(), calls=%async_computation.1 | async-start | bytes 655360 | tf_op jit(solution)/shard_map/reduce_scatter | solution.py:114
  8.7 5.8 %copy-start.12 = (f32[1,1,128,16]{2,3,1,0:T(8,128)S(1)}, f32[1,1,128,16]{2,3,1,0:T(8,128)}, u32[]{:S(2)}) copy-start(f32[1,1,128,16]{2,3,1,0:T(8,128)} %param.16) | copy-start | bytes 24580
  10.9 3.8 %copy-start.13 = (f32[1,16]{1,0:T(1,128)S(1)}, f32[1,16]{1,0:T(1,128)}, u32[]{:S(2)}) copy-start(f32[1,16]{1,0:T(1,128)} %param.19) | copy-start | bytes 196
  10.9 4.0 %copy-start.10 = (bf16[1,1,128,128]{3,2,1,0:T(8,128)(2,1)S(1)}, bf16[1,1,128,128]{3,2,1,0:T(8,128)(2,1)}, u32[]{:S(2)}) copy-start(bf16[1,1,128,128]{3,2,1,0:T(8,128)(2,1)} %param.12) | copy-start | bytes 98308
  10.9 19.0 %copy-start.11 = (bf16[1,1,128,128]{3,2,1,0:T(8,128)(2,1)S(1)}, bf16[1,1,128,128]{3,2,1,0:T(8,128)(2,1)}, u32[]{:S(2)}) copy-start(bf16[1,1,128,128]{3,2,1,0:T(8,128)(2,1)} %param.13) | copy-start | bytes 98308
  12.1 33.3 %copy-start.7 = (bf16[1,1,128,2048]{3,2,1,0:T(8,128)(2,1)S(1)}, bf16[1,1,128,2048]{3,2,1,0:T(8,128)(2,1)}, u32[]{:S(2)}) copy-start(bf16[1,1,128,2048]{3,2,1,0:T(8,128)(2,1)} %param.15) | copy-start | bytes 1572868
  45.5 1.3 copy-start.1
  45.6 5.5 %copy-start.14 = (s32[1,1,2,16]{3,2,1,0:T(2,128)S(1)}, s32[1,1,2,16]{3,2,1,0:T(2,128)}, u32[]{:S(2)}) copy-start(s32[1,1,2,16]{3,2,1,0:T(2,128)} %param.17) | copy-start | bytes 388
  52.1 2.6 %copy-start.8 = (bf16[2,1024,128]{2,1,0:T(8,128)(2,1)S(1)}, bf16[2,1024,128]{2,1,0:T(8,128)(2,1)}, u32[]{:S(2)}) copy-start(bf16[2,1024,128]{2,1,0:T(8,128)(2,1)} %get-tuple-element.221) | copy-start | bytes 1572868 | tf_op jit(solution)/shard_map/while
  54.8 2.3 %copy-start.5 = (f32[2,1024,128]{2,1,0:T(8,128)S(1)}, f32[2,1024,128]{2,1,0:T(8,128)}, u32[]{:S(2)}) copy-start(f32[2,1024,128]{2,1,0:T(8,128)} %get-tuple-element.200) | copy-start | bytes 3145732 | tf_op jit(solution)/shard_map/while
  57.0 1.2 copy-start.2
  58.3 1.0 copy-start.6
  59.3 1.0 copy-start.3
  61.3 2.6 %copy-start.8 = (bf16[2,1024,128]{2,1,0:T(8,128)(2,1)S(1)}, bf16[2,1024,128]{2,1,0:T(8,128)(2,1)}, u32[]{:S(2)}) copy-start(bf16[2,1024,128]{2,1,0:T(8,128)(2,1)} %get-tuple-element.221) | copy-start | bytes 1572868 | tf_op jit(solution)/shard_map/while
  63.9 2.3 %copy-start.5 = (f32[2,1024,128]{2,1,0:T(8,128)S(1)}, f32[2,1024,128]{2,1,0:T(8,128)}, u32[]{:S(2)}) copy-start(f32[2,1024,128]{2,1,0:T(8,128)} %get-tuple-element.200) | copy-start | bytes 3145732 | tf_op jit(solution)/shard_map/while
  66.2 1.2 copy-start.2
  67.4 1.0 copy-start.6
  68.4 1.0 copy-start.3
  71.1 3.3 %copy-start.4 = (f32[2,1024,128]{2,1,0:T(8,128)S(1)}, f32[2,1024,128]{2,1,0:T(8,128)}, u32[]{:S(2)}) copy-start(f32[2,1024,128]{2,1,0:T(8,128)} %get-tuple-element.69) | copy-start | bytes 3145732
  75.4 45.3 %collective-permute-start = (bf16[128,2048]{1,0:T(8,128)(2,1)S(1)}, bf16[128,2048]{1,0:T(8,128)(2,1)}, u32[]{:S(2)}, u32[]{:S(2)}) collective-permute-start(bf16[128,2048]{1,0:T(8,128)(2,1)S(1)} %fusion.37), channel_id=1, source_target_pairs={{4,0},{5,1},{6,2},{7,3},{12,8},{13,9},{14,10},{15,11},{20,16},{21,... | collective-permute-start | bytes 1572872 | tf_op jit(solution)/shard_map/ppermute | solution.py:18
  98.1 22.7 %collective-permute-start.2 = (bf16[128,128]{1,0:T(8,128)(2,1)S(1)}, bf16[128,128]{1,0:T(8,128)(2,1)S(1)}, u32[]{:S(2)}, u32[]{:S(2)}) collective-permute-start(bf16[128,128]{1,0:T(8,128)(2,1)S(1)} %get-tuple-element.106), channel_id=1, source_target_pairs={{4,0},{5,1},{6,2},{7,3},{12,8},{13,9},{14,10},{15,11},{20,16},{21,... | collective-permute-start | bytes 98312 | tf_op jit(solution)/shard_map/ppermute | solution.py:18
  99.4 21.4 %collective-permute-start.1 = (bf16[128,128]{1,0:T(8,128)(2,1)S(1)}, bf16[128,128]{1,0:T(8,128)(2,1)S(1)}, u32[]{:S(2)}, u32[]{:S(2)}) collective-permute-start(bf16[128,128]{1,0:T(8,128)(2,1)S(1)} %get-tuple-element.107), channel_id=1, source_target_pairs={{4,0},{5,1},{6,2},{7,3},{12,8},{13,9},{14,10},{15,11},{20,16},{21,... | collective-permute-start | bytes 98312 | tf_op jit(solution)/shard_map/ppermute | solution.py:18
Sparse Core Ops, SparseCore 0:
  74.2 22.9 reduce-scatter.1
